TPU v7x, 768 devices: a whole 4x8x12 slice. The times are simulated.
768 devices in a mesh: tiles: 192 (over y, z, core), band: 4 (over x).
Axes of the slice: x: 4, y: 8, z: 12, core: 2. Of those that a mesh axis runs over, the one named last changes fastest.
Arguments:
- optical_depth: bfloat16 [3072, 90, 4, 512], P('tiles', None, None, 'band'), may hold values from 0.00049972534 to 0.029907227
- albedo: bfloat16 [3072, 90, 512], P('tiles', None, 'band'), may hold values from 0.69921875 to 0.96875
- insolation: bfloat16 [3072, 512], P('tiles', 'band'), may hold values from 20 to 100
- sunlit: int32 [3072, 4], P('tiles', 'band'), may hold values from 0 to 1, as said below
- point_weight: float32 [4], replicated, may hold values from 0.1 to 1
- anomaly: float32 [3072, 90, 512], P('tiles', None, 'band'), may hold values from -6 to 6
Outputs:
- heating: float32 [3072, 90, 512], P('tiles', None, 'band')
- smoothed: float32 [3072, 90, 512], P('tiles', None, 'band')
Inputs may be any that keep to these rules, and one draw needn't show every extreme that they name: In every row, of two blocks that lie half of 4 sectors apart, exactly one is sunlit.
All inputs are finite; a program needn't handle non-finite values.
Results may differ from a plain program's by a relative error of at most 0.00045.
Values may be sent and summed in bfloat16 or wider, within the bound.
No kernel may reach another device: no remote copies, remote signals or barrier semaphores. Data moves between devices by JAX's collectives and lax.ppermute only.
A program may use at most 64 MiB of HBM per device.

v0:
```python
import functools
import math

import jax
import jax.numpy as jnp
from jax import lax
from jax.experimental import pallas as pl
from jax.experimental.pallas import tpu as pltpu
from jax.sharding import PartitionSpec as P

DIFF_STEPS = 4
BATCH = 18
GROUPS = 12
UNROLL_DOWN = 5
UNROLL_UP = 6
LIGHT_RATE = -2.0 * math.log2(math.e)
HALO = 4
EDGE = 16
SUB = 8
F32 = jnp.float32
BF16 = jnp.bfloat16
base_loss = 0.005
step_scale = 0.2**DIFF_STEPS


def vmem():
    return pl.BlockSpec(memory_space=pltpu.VMEM)


def smem():
    return pl.BlockSpec(memory_space=pltpu.SMEM)


def radiate_kernel(
    here_ref, weight_ref, lit_ref, depth_ref, albedo_ref, sun_ref, anomaly_ref,
    heat_ref, field_ref, pair_ref, step_ref,
    spread_ref, ratio_ref, swept_ref, extinct_ref,
):
    rows, levels, points, width = depth_ref.shape
    per_level = rows * points
    halves = rows // SUB
    chains = halves * points
    sun = sun_ref[...].astype(F32)
    row_ids = lax.broadcasted_iota(jnp.int32, (rows, width), 0)
    lit = jnp.zeros((rows, width), jnp.int32)
    for row in range(rows):
        lit = jnp.where(row_ids == row, lit_ref[row], lit)
    sun = jnp.where(lit == 1, sun, 0.0)
    suns = [sun[h * SUB:(h + 1) * SUB] for h in range(halves)]
    weights = [weight_ref[point] for point in range(points)]

    def spread(level):
        for row in range(rows):
            spread_ref[pl.ds(level * per_level + points * row, points), :] = (
                depth_ref[row, level].astype(F32)
            )

    def depth_of(level, half, point):
        start = level * per_level + half * SUB * points + point
        return spread_ref[pl.ds(start, SUB, stride=points), :]

    def albedo_of(level):
        both = albedo_ref[level].astype(F32)
        return [both[h * SUB:(h + 1) * SUB] for h in range(halves)]

    def place(level, chain):
        return pl.ds(pl.multiple_of(level * per_level + chain * SUB, SUB), SUB)

    zero = jnp.zeros((SUB, width), F32)
    one = jnp.ones((SUB, width), F32)

    def down(level, carry):
        link_prev, albedo_now, depth, light, ratio, swept = carry
        last = level == levels - 1
        following = jnp.where(last, level, level + 1)
        spread(following)
        albedo_next = albedo_of(following)
        out = ([], [], [], [], [])
        for half in range(halves):
            albedo = albedo_now[half]
            before = link_prev[half]
            link = jnp.where(last, 0.0, albedo * albedo_next[half])
            slope = 2.0 * (1.0 - albedo)
            level_part = base_loss + before + link
            direct = None
            for point in range(points):
                chain = half * points + point
                layer = depth_of(level, half, point)
                depth_new = depth[chain] + layer
                light_new = jnp.exp2(depth_new * LIGHT_RATE)
                extinct = weights[point] * (light[chain] - light_new)
                direct = extinct if direct is None else direct + extinct
                inverse = 1.0 / (level_part + slope * layer - before * ratio[chain])
                ratio_new = link * inverse
                swept_new = (albedo * extinct + before * swept[chain]) * inverse
                where = place(level, chain)
                ratio_ref[where, :] = ratio_new
                swept_ref[where, :] = swept_new
                for item, value in zip(out, (depth_new, light_new, ratio_new, swept_new)):
                    item.append(value)
            out[4].append(link)
            extinct_ref[level, pl.ds(half * SUB, SUB), :] = direct
        return (
            tuple(out[4]), tuple(albedo_next), tuple(out[0]), tuple(out[1]), tuple(out[2]),
            tuple(out[3]),
        )

    spread(0)
    lax.fori_loop(
        0, levels, down,
        ((zero,) * halves, tuple(albedo_of(0)), (zero,) * chains, (one,) * chains,
         (zero,) * chains, (zero,) * chains),
        unroll=UNROLL_DOWN,
    )
    even = here_ref[0] % 2 == 0

    def up(i, flux):
        level = levels - 1 - i
        albedos = albedo_of(level)
        flux_new = []
        fields = []
        for half in range(halves):
            total = None
            for point in range(points):
                chain = half * points + point
                where = place(level, chain)
                diffuse = swept_ref[where, :] + ratio_ref[where, :] * flux[chain]
                flux_new.append(diffuse)
                term = depth_of(level, half, point) * diffuse
                total = term if total is None else total + term
            part = pl.ds(half * SUB, SUB)
            absorbed = extinct_ref[level, part, :] + 2.0 * total
            heat = suns[half] * ((1.0 - albedos[half]) * absorbed)
            heat_ref[level, part, :] = heat
            field = anomaly_ref[level, part, :] + heat
            field_ref[level, part, :] = field
            fields.append(field)
        top, bottom = fields[0][:HALO], fields[-1][SUB - HALO:]
        pair_ref[level] = jnp.where(even, bottom, top).astype(BF16)
        step_ref[level] = jnp.where(even, top, bottom).astype(BF16)
        return tuple(flux_new)

    lax.fori_loop(0, levels, up, (zero,) * chains, unroll=UNROLL_UP)


def outer_rows(here_ref, pair_ref, step_ref, level):
    pair, step = pair_ref[level].astype(F32), step_ref[level].astype(F32)
    even = here_ref[0] % 2 == 0
    below = jnp.where(even, pair, step)
    above = jnp.where(even, step, pair)
    return jnp.concatenate([below, above], axis=0)


def pack_levels(lanes, parts):
    width = lanes.shape[1]
    packed = None
    for slot, part in enumerate(parts):
        moved = pltpu.roll(part, (EDGE * slot + EDGE // 2) % width, 1)
        packed = moved if packed is None else jnp.where(lanes >= EDGE * slot, moved, packed)
    return packed


def each_block(levels, per_group, body):
    full = levels // per_group
    counts = [per_group] * full + ([levels % per_group] if levels % per_group else [])
    blocks = full // GROUPS
    lax.fori_loop(0, blocks, lambda b, c: (body(b, counts[:GROUPS]), c)[1], 0)
    if counts[blocks * GROUPS:]:
        body(blocks, counts[blocks * GROUPS:])


def pack_own_kernel(field_ref, packed_ref):
    levels, rows, width = field_ref.shape
    per_group = width // EDGE
    lanes = lax.broadcasted_iota(jnp.int32, (SUB, width), 1)

    def block_of(block, counts):
        for i, count in enumerate(counts):
            group = block * GROUPS + i
            for half in range(rows // SUB):
                where = pl.ds(half * SUB, SUB)
                packed_ref[group, where, :] = pack_levels(
                    lanes, [field_ref[group * per_group + k, where, :] for k in range(count)]
                )

    each_block(levels, per_group, block_of)


def pack_outer_kernel(
    here_ref, side_ref, pair_ref, step_ref, own_ref, outer_ref, near_ref, far_ref
):
    levels, _, width = pair_ref.shape
    halves = own_ref.shape[1] // SUB
    per_group = width // EDGE
    lanes = lax.broadcasted_iota(jnp.int32, (SUB, width), 1)
    mid = EDGE // 2
    lower = lanes % EDGE < mid
    even = side_ref[0] % 2 == 0

    def block_of(block, counts):
        packed = []
        for i, count in enumerate(counts):
            group = block * GROUPS + i
            outer = pack_levels(
                lanes,
                [outer_rows(here_ref, pair_ref, step_ref, group * per_group + k)
                 for k in range(count)],
            )
            outer_ref[group] = outer
            packed.append(
                [own_ref[group, pl.ds(h * SUB, SUB), :] for h in range(halves)] + [outer]
            )
        for i in range(0, len(counts), 2):
            for part, (x, y) in enumerate(zip(packed[i], packed[i + 1])):
                last = jnp.where(lower, x, pltpu.roll(y, mid, 1))
                first = jnp.where(lower, pltpu.roll(x, width - mid, 1), y)
                both = block * (GROUPS // 2) + i // 2
                where = pl.ds(part * SUB, SUB)
                near_ref[both, where, :] = jnp.where(even, last, first).astype(BF16)
                far_ref[both, where, :] = jnp.where(even, first, last).astype(BF16)

    each_block(levels, per_group, block_of)


def around(parts, first, final):
    down = [pltpu.roll(x, 1, 0) for x in parts]
    up = [pltpu.roll(x, SUB - 1, 0) for x in parts]
    count = len(parts)
    return [
        jnp.where(first, down[i - 1], down[i]) + jnp.where(final, up[(i + 1) % count], up[i])
        for i in range(count)
    ]


def inside(here_ref, tiles, width):
    sub = lax.broadcasted_iota(jnp.int32, (SUB, width), 0)
    tile = here_ref[0]
    keep = jnp.where(
        sub < HALO, (tile < tiles - 1).astype(jnp.int32), (tile > 0).astype(jnp.int32)
    )
    return sub == 0, sub == SUB - 1, keep.astype(F32)


def main_kernel(tiles, here_ref, field_ref, pair_ref, step_ref, out_ref):
    levels, rows, width = field_ref.shape
    first, final, keep = inside(here_ref, tiles, width)

    def some_levels(block, carry):
        found = [block * BATCH + i for i in range(BATCH)]
        sets = [
            [field_ref[level, pl.ds(h * SUB, SUB), :] for h in range(rows // SUB)]
            + [outer_rows(here_ref, pair_ref, step_ref, level)]
            for level in found
        ]
        for _ in range(DIFF_STEPS):
            new = []
            for parts in sets:
                vertical = around(parts, first, final)
                parts = [
                    x + v + (pltpu.roll(x, 1, 1) + pltpu.roll(x, width - 1, 1))
                    for x, v in zip(parts, vertical)
                ]
                parts[-1] = parts[-1] * keep
                new.append(parts)
            sets = new
        for level, parts in zip(found, sets):
            for half, value in enumerate(parts[:-1]):
                out_ref[level, pl.ds(half * SUB, SUB), :] = value * step_scale
        return carry

    lax.fori_loop(0, levels // BATCH, some_levels, 0)


def edge_kernel(
    tiles, here_ref, side_ref, own_ref, outer_ref, near_ref, far_ref, main_ref, out_ref
):
    levels, rows, width = main_ref.shape
    per_group = width // EDGE
    halves = rows // SUB
    first, final, keep = inside(here_ref, tiles, width)
    even = side_ref[0] % 2 == 0
    lanes = lax.broadcasted_iota(jnp.int32, (SUB, width), 1)
    column = lanes % EDGE
    mid = EDGE // 2
    last_own = column == mid - 1
    first_own = column == mid
    lower = column < mid
    touched = (lanes < HALO) | (lanes >= width - HALO)

    def block_of(block, counts):
        groups = [block * GROUPS + i for i in range(len(counts))]
        sets = [
            ([own_ref[group, pl.ds(h * SUB, SUB), :] for h in range(halves)]
             + [outer_ref[group]], [])
            for group in groups
        ]
        for i in range(0, len(groups), 2):
            both = block * (GROUPS // 2) + i // 2
            for part in range(halves + 1):
                where = pl.ds(part * SUB, SUB)
                near = near_ref[both, where, :].astype(F32)
                far = far_ref[both, where, :].astype(F32)
                west, east = jnp.where(even, far, near), jnp.where(even, near, far)
                sets[i][1].append(jnp.where(lower, west, pltpu.roll(east, mid, 1)))
                sets[i + 1][1].append(jnp.where(lower, pltpu.roll(west, width - mid, 1), east))
        for _ in range(DIFF_STEPS):
            new = []
            for own, other in sets:
                own_rows = around(own, first, final)
                other_rows = around(other, first, final)
                own_new, other_new = [], []
                for x, y, v, u in zip(own, other, own_rows, other_rows):
                    xe, ye = pltpu.roll(x, width - 1, 1), pltpu.roll(y, width - 1, 1)
                    xw, yw = pltpu.roll(x, 1, 1), pltpu.roll(y, 1, 1)
                    own_new.append(
                        x + v + (jnp.where(first_own, yw, xw) + jnp.where(last_own, ye, xe))
                    )
                    other_new.append(
                        y + u + (jnp.where(first_own, xw, yw) + jnp.where(last_own, xe, ye))
                    )
                own_new[-1] = own_new[-1] * keep
                other_new[-1] = other_new[-1] * keep
                new.append((own_new, other_new))
            sets = new
        for group, count, (own, _) in zip(groups, counts, sets):
            for half in range(halves):
                scaled = own[half] * step_scale
                where = pl.ds(half * SUB, SUB)
                for slot in range(count):
                    moved = pltpu.roll(scaled, (width - EDGE * slot - mid) % width, 1)
                    level = group * per_group + slot
                    out_ref[level, where, :] = jnp.where(
                        touched, moved, main_ref[level, where, :]
                    )

    each_block(levels, per_group, block_of)


def fast(shape, dtype):
    return pltpu.VMEM(shape, dtype)


def held(x):
    return pltpu.with_memory_space_constraint(x, pltpu.VMEM)


def swaps(size, first, ring):
    ends = range(first, size if ring else size - 1, 2)
    return [pair for i in ends for pair in ((i, (i + 1) % size), ((i + 1) % size, i))]


def per_device(optical_depth, albedo, insolation, sunlit, point_weight, anomaly):
    rows, levels, points, width = optical_depth.shape
    tiles, bands = lax.axis_size("tiles"), lax.axis_size("band")
    here = lax.axis_index("tiles").astype(jnp.int32).reshape(1)
    side = lax.axis_index("band").astype(jnp.int32).reshape(1)
    planes = (levels, rows, width)
    edges = (levels, HALO, width)
    groups = -(-levels * EDGE // width)
    groups += groups % 2
    sweep = pltpu.VMEM((levels * rows * points, width), F32)
    heat, field, pair_edge, step_edge = pl.pallas_call(
        radiate_kernel,
        in_specs=[smem(), smem(), smem(), vmem(), vmem(), vmem(), vmem()],
        out_specs=[vmem()] * 4,
        out_shape=[
            jax.ShapeDtypeStruct(planes, F32), fast(planes, F32), fast(edges, BF16),
            fast(edges, BF16),
        ],
        scratch_shapes=[sweep] * 3 + [pltpu.VMEM(planes, F32)],
        name="radiate",
    )(
        here, point_weight, sunlit.reshape(rows), optical_depth, jnp.swapaxes(albedo, 0, 1),
        insolation, jnp.swapaxes(anomaly, 0, 1),
    )
    from_step = lax.ppermute(step_edge, "tiles", swaps(tiles, 1, False))
    from_pair = lax.ppermute(pair_edge, "tiles", swaps(tiles, 0, False))
    own = pl.pallas_call(
        pack_own_kernel,
        in_specs=[vmem()],
        out_specs=vmem(),
        out_shape=fast((groups, rows, width), F32),
        name="pack_own",
    )(held(field))
    sent = fast((groups // 2, rows + SUB, width), BF16)
    outer, to_near, to_far = pl.pallas_call(
        pack_outer_kernel,
        in_specs=[smem(), smem()] + [vmem()] * 3,
        out_specs=[vmem()] * 3,
        out_shape=[fast((groups, SUB, width), F32), sent, sent],
        name="pack_outer",
    )(here, side, held(from_pair), held(from_step), held(own))
    far = lax.ppermute(to_far, "band", swaps(bands, 1, True))
    near = lax.ppermute(to_near, "band", swaps(bands, 0, True))
    inner = pl.pallas_call(
        functools.partial(main_kernel, tiles),
        in_specs=[smem()] + [vmem()] * 3,
        out_specs=vmem(),
        out_shape=fast(planes, F32),
        name="inner",
    )(here, held(field), held(from_pair), held(from_step))
    smoothed = pl.pallas_call(
        functools.partial(edge_kernel, tiles),
        in_specs=[smem(), smem()] + [vmem()] * 5,
        out_specs=vmem(),
        out_shape=jax.ShapeDtypeStruct(planes, F32),
        name="edge",
    )(here, side, held(own), held(outer), held(near), held(far), held(inner))
    return jnp.swapaxes(heat, 0, 1), jnp.swapaxes(smoothed, 0, 1)


def solution(mesh):
    placed = (
        P("tiles", None, None, "band"),
        P("tiles", None, "band"),
        P("tiles", "band"),
        P("tiles", "band"),
        P(),
        P("tiles", None, "band"),
    )
    return jax.shard_map(
        per_device,
        mesh=mesh,
        in_specs=placed,
        out_specs=(P("tiles", None, "band"), P("tiles", None, "band")),
        check_vma=False,
    )
```

profile of v0, /device:TPU:48, one launch (start us, length us, event | category | flops | bytes accessed | tf_op | source)
XLA Modules:
  0.0 38.2 jit_solution(1173639973366910075)
XLA Ops:
  0.6 5.5 %radiate.1 = (f32[90,16,128]{2,1,0:T(8,128)}, f32[90,16,128]{2,1,0:T(8,128)S(1)}, bf16[90,4,128]{2,1,0:T(4,128)(2,1)S(1)}, bf16[90,4,128]{2,1,0:T(4,128)(2,1)S(1)}) custom-call(s32[1]{0:T(128)} %bitcast.here_ref, f32[4]{0:T(128)} %weight_ref.1, s32[16]{0:T(128)} %bitcast.10, bf16[16,90,4,128]{3,2,1,0:T(4,128)(2,1)} %depth_ref.1, ...), custom_call_target="tpu_custom_call" | custom-call | tf_op jit(solution)/shard_map/radiate/pallas_call | solution.py:362
  6.1 1.9 %collective-permute-start = (bf16[90,4,128]{2,1,0:T(4,128)(2,1)S(1)}, bf16[90,4,128]{2,1,0:T(4,128)(2,1)S(1)}, u32[]{:S(2)}, u32[]{:S(2)}) collective-permute-start(bf16[90,4,128]{2,1,0:T(4,128)(2,1)S(1)} %get-tuple-element.11), channel_id=1, source_target_pairs={{0,4},{4,0},{8,12},{12,8},{16,20},{20,16},{24,28},{28,24},{32,36},... | collective-permute-start | bytes 276488 | tf_op jit(solution)/shard_map/ppermute | solution.py:377
  8.0 15.5 %collective-permute-start.1 = (bf16[90,4,128]{2,1,0:T(4,128)(2,1)S(1)}, bf16[90,4,128]{2,1,0:T(4,128)(2,1)S(1)}, u32[]{:S(2)}, u32[]{:S(2)}) collective-permute-start(bf16[90,4,128]{2,1,0:T(4,128)(2,1)S(1)} %get-tuple-element.12), channel_id=1, source_target_pairs={{4,8},{8,4},{12,16},{16,12},{20,24},{24,20},{28,32},{32,28},{36,40... | collective-permute-start | bytes 276488 | tf_op jit(solution)/shard_map/ppermute | solution.py:376
  23.5 0.3 pack_own.1.own_ref
  23.8 0.0 collective-permute-done.pair_ref
  23.8 1.9 %collective-permute-done.1.step_ref = bf16[90,4,128]{2,1,0:T(4,128)(2,1)S(1)} collective-permute-done((bf16[90,4,128]{2,1,0:T(4,128)(2,1)S(1)}, bf16[90,4,128]{2,1,0:T(4,128)(2,1)S(1)}, u32[]{:S(2)}, u32[]{:S(2)}) %collective-permute-start.1) | collective-permute-done | bytes 92192 | tf_op jit(solution)/shard_map/ppermute | solution.py:376
  25.7 0.2 pack_outer.1
  26.0 3.4 %collective-permute-start.2 = (bf16[6,24,128]{2,1,0:T(8,128)(2,1)S(1)}, bf16[6,24,128]{2,1,0:T(8,128)(2,1)S(1)}, u32[]{:S(2)}, u32[]{:S(2)}) collective-permute-start(bf16[6,24,128]{2,1,0:T(8,128)(2,1)S(1)} %get-tuple-element.14), channel_id=1, source_target_pairs={{0,1},{1,0},{2,3},{3,2},{4,5},{5,4},{6,7},{7,6},{8,9},{9,8},{10,11... | collective-permute-start | bytes 110600 | tf_op jit(solution)/shard_map/ppermute | solution.py:394
  29.4 4.0 %collective-permute-start.3 = (bf16[6,24,128]{2,1,0:T(8,128)(2,1)S(1)}, bf16[6,24,128]{2,1,0:T(8,128)(2,1)S(1)}, u32[]{:S(2)}, u32[]{:S(2)}) collective-permute-start(bf16[6,24,128]{2,1,0:T(8,128)(2,1)S(1)} %get-tuple-element.15), channel_id=1, source_target_pairs={{1,2},{2,1},{3,0},{0,3},{5,6},{6,5},{7,4},{4,7},{9,10},{10,9},{11,... | collective-permute-start | bytes 110600 | tf_op jit(solution)/shard_map/ppermute | solution.py:393
  33.4 2.4 %inner.1.main_ref = f32[90,16,128]{2,1,0:T(8,128)S(1)} custom-call(s32[1]{0:T(128)} %bitcast.here_ref, f32[90,16,128]{2,1,0:T(8,128)S(1)} %get-tuple-element.10.field_ref, bf16[90,4,128]{2,1,0:T(4,128)(2,1)S(1)} %collective-permute-done.pair_ref, bf16[90,4,128]{2,1,0:T(4,128)(2,1)S(1)} %collective-permute-done.1.step_ref), custom_call_target="tpu_custom_call" | custom-call | tf_op jit(solution)/shard_map/inner/pallas_call | solution.py:395
  35.7 0.0 collective-permute-done.2.near_ref
  35.8 0.7 %collective-permute-done.3.far_ref = bf16[6,24,128]{2,1,0:T(8,128)(2,1)S(1)} collective-permute-done((bf16[6,24,128]{2,1,0:T(8,128)(2,1)S(1)}, bf16[6,24,128]{2,1,0:T(8,128)(2,1)S(1)}, u32[]{:S(2)}, u32[]{:S(2)}) %collective-permute-start.3) | collective-permute-done | bytes 36896 | tf_op jit(solution)/shard_map/ppermute | solution.py:393
  36.4 1.7 %edge.1 = f32[90,16,128]{2,1,0:T(8,128)} custom-call(s32[1]{0:T(128)} %bitcast.here_ref, s32[1]{0:T(128)} %bitcast.5.side_ref, f32[12,16,128]{2,1,0:T(8,128)S(1)} %pack_own.1.own_ref, f32[12,8,128]{2,1,0:T(8,128)S(1)} %get-tuple-element.13.outer_ref, bf16[6,24,128]{2,1,0:T(8,128)(2,1)S(1)} %collective-permute-done.2.near_ref, ...), custom_call_target="tpu_custom_call" | custom-call | tf_op jit(solution)/shard_map/edge/pallas_call | solution.py:402
Async XLA Ops:
  6.1 17.7 %collective-permute-start = (bf16[90,4,128]{2,1,0:T(4,128)(2,1)S(1)}, bf16[90,4,128]{2,1,0:T(4,128)(2,1)S(1)}, u32[]{:S(2)}, u32[]{:S(2)}) collective-permute-start(bf16[90,4,128]{2,1,0:T(4,128)(2,1)S(1)} %get-tuple-element.11), channel_id=1, source_target_pairs={{0,4},{4,0},{8,12},{12,8},{16,20},{20,16},{24,28},{28,24},{32,36},... | collective-permute-start | bytes 276488 | tf_op jit(solution)/shard_map/ppermute | solution.py:377
  8.0 17.7 %collective-permute-start.1 = (bf16[90,4,128]{2,1,0:T(4,128)(2,1)S(1)}, bf16[90,4,128]{2,1,0:T(4,128)(2,1)S(1)}, u32[]{:S(2)}, u32[]{:S(2)}) collective-permute-start(bf16[90,4,128]{2,1,0:T(4,128)(2,1)S(1)} %get-tuple-element.12), channel_id=1, source_target_pairs={{4,8},{8,4},{12,16},{16,12},{20,24},{24,20},{28,32},{32,28},{36,40... | collective-permute-start | bytes 276488 | tf_op jit(solution)/shard_map/ppermute | solution.py:376
  26.0 9.8 %collective-permute-start.2 = (bf16[6,24,128]{2,1,0:T(8,128)(2,1)S(1)}, bf16[6,24,128]{2,1,0:T(8,128)(2,1)S(1)}, u32[]{:S(2)}, u32[]{:S(2)}) collective-permute-start(bf16[6,24,128]{2,1,0:T(8,128)(2,1)S(1)} %get-tuple-element.14), channel_id=1, source_target_pairs={{0,1},{1,0},{2,3},{3,2},{4,5},{5,4},{6,7},{7,6},{8,9},{9,8},{10,11... | collective-permute-start | bytes 110600 | tf_op jit(solution)/shard_map/ppermute | solution.py:394
  29.4 7.1 %collective-permute-start.3 = (bf16[6,24,128]{2,1,0:T(8,128)(2,1)S(1)}, bf16[6,24,128]{2,1,0:T(8,128)(2,1)S(1)}, u32[]{:S(2)}, u32[]{:S(2)}) collective-permute-start(bf16[6,24,128]{2,1,0:T(8,128)(2,1)S(1)} %get-tuple-element.15), channel_id=1, source_target_pairs={{1,2},{2,1},{3,0},{0,3},{5,6},{6,5},{7,4},{4,7},{9,10},{10,9},{11,... | collective-permute-start | bytes 110600 | tf_op jit(solution)/shard_map/ppermute | solution.py:393
where the time goes:
time: 38.4 us; the launch traced here: 38.2 us
  starting transfers between devices  24.8 us (65%)
  Pallas kernels  10 us (26%)
  waiting for transfers between devices  2.63 us (7%)
  between operations  0.7 us (2%)
    ppermute x1, starting transfers between devices, per_device(): from_step = lax.ppermute(step_edge, 'tiles', swaps(tiles, 1, False))  15.5 us
    pallas_call x1, Pallas kernels, per_device(): pl.pallas_call(radiate_kernel, in_specs=[smem(), smem(), smem(), vmem(),...  5.48 us
    ppermute x1, starting transfers between devices, per_device(): far = lax.ppermute(to_far, 'band', swaps(bands, 1, True))  4 us
    ppermute x1, starting transfers between devices, per_device(): near = lax.ppermute(to_near, 'band', swaps(bands, 0, True))  3.39 us
    pallas_call x1, Pallas kernels, per_device(): pl.pallas_call(functools.partial(main_kernel, tiles), in_specs=[smem()] +...  2.36 us
    ppermute x1, waiting for transfers between devices, per_device(): from_step = lax.ppermute(step_edge, 'tiles', swaps(tiles, 1, False))  1.95 us
    ppermute x1, starting transfers between devices, per_device(): from_pair = lax.ppermute(pair_edge, 'tiles', swaps(tiles, 0, False))  1.91 us
    pallas_call x1, Pallas kernels, per_device(): pl.pallas_call(functools.partial(edge_kernel, tiles), in_specs=[smem(), s...  1.72 us
  transfers between devices with their start and end apart: 4, of which 2 were waited for; matrix products, arithmetic and copies ran while one was open for 0% of the time, Pallas kernels for 7%

commit v1 on v0

--- a/solution.py
+++ b/solution.py
@@ -9,6 +9,7 @@
 from jax.sharding import PartitionSpec as P
 
 DIFF_STEPS = 4
+RING = 24
 BATCH = 18
 GROUPS = 12
 UNROLL_DOWN = 5
@@ -143,8 +144,9 @@
     lax.fori_loop(0, levels, up, (zero,) * chains, unroll=UNROLL_UP)
 
 
-def outer_rows(here_ref, pair_ref, step_ref, level):
-    pair, step = pair_ref[level].astype(F32), step_ref[level].astype(F32)
+def outer_rows(here_ref, pair_ref, late_ref, step_ref, level):
+    pair = pair_ref[level].astype(F32) + late_ref[level].astype(F32)
+    step = step_ref[level].astype(F32)
     even = here_ref[0] % 2 == 0
     below = jnp.where(even, pair, step)
     above = jnp.where(even, step, pair)
@@ -187,7 +189,7 @@
 
 
 def pack_outer_kernel(
-    here_ref, side_ref, pair_ref, step_ref, own_ref, outer_ref, near_ref, far_ref
+    here_ref, side_ref, pair_ref, late_ref, step_ref, own_ref, outer_ref, near_ref, far_ref
 ):
     levels, _, width = pair_ref.shape
     halves = own_ref.shape[1] // SUB
@@ -203,7 +205,7 @@
             group = block * GROUPS + i
             outer = pack_levels(
                 lanes,
-                [outer_rows(here_ref, pair_ref, step_ref, group * per_group + k)
+                [outer_rows(here_ref, pair_ref, late_ref, step_ref, group * per_group + k)
                  for k in range(count)],
             )
             outer_ref[group] = outer
@@ -241,7 +243,7 @@
     return sub == 0, sub == SUB - 1, keep.astype(F32)
 
 
-def main_kernel(tiles, here_ref, field_ref, pair_ref, step_ref, out_ref):
+def main_kernel(tiles, here_ref, field_ref, pair_ref, late_ref, step_ref, out_ref):
     levels, rows, width = field_ref.shape
     first, final, keep = inside(here_ref, tiles, width)
 
@@ -249,7 +251,7 @@
         found = [block * BATCH + i for i in range(BATCH)]
         sets = [
             [field_ref[level, pl.ds(h * SUB, SUB), :] for h in range(rows // SUB)]
-            + [outer_rows(here_ref, pair_ref, step_ref, level)]
+            + [outer_rows(here_ref, pair_ref, late_ref, step_ref, level)]
             for level in found
         ]
         for _ in range(DIFF_STEPS):
@@ -374,7 +376,9 @@
         insolation, jnp.swapaxes(anomaly, 0, 1),
     )
     from_step = lax.ppermute(step_edge, "tiles", swaps(tiles, 1, False))
-    from_pair = lax.ppermute(pair_edge, "tiles", swaps(tiles, 0, False))
+    pairs = swaps(tiles, 0, False)
+    from_pair = lax.ppermute(pair_edge, "tiles", [p for p in pairs if p[0] % RING < RING // 2])
+    from_late = lax.ppermute(pair_edge, "tiles", [p for p in pairs if p[0] % RING >= RING // 2])
     own = pl.pallas_call(
         pack_own_kernel,
         in_specs=[vmem()],
@@ -385,20 +389,20 @@
     sent = fast((groups // 2, rows + SUB, width), BF16)
     outer, to_near, to_far = pl.pallas_call(
         pack_outer_kernel,
-        in_specs=[smem(), smem()] + [vmem()] * 3,
+        in_specs=[smem(), smem()] + [vmem()] * 4,
         out_specs=[vmem()] * 3,
         out_shape=[fast((groups, SUB, width), F32), sent, sent],
         name="pack_outer",
-    )(here, side, held(from_pair), held(from_step), held(own))
+    )(here, side, held(from_pair), held(from_late), held(from_step), held(own))
+    near = lax.ppermute(to_near, "band", swaps(bands, 0, True))
     far = lax.ppermute(to_far, "band", swaps(bands, 1, True))
-    near = lax.ppermute(to_near, "band", swaps(bands, 0, True))
     inner = pl.pallas_call(
         functools.partial(main_kernel, tiles),
-        in_specs=[smem()] + [vmem()] * 3,
+        in_specs=[smem()] + [vmem()] * 4,
         out_specs=vmem(),
         out_shape=fast(planes, F32),
         name="inner",
-    )(here, held(field), held(from_pair), held(from_step))
+    )(here, held(field), held(from_pair), held(from_late), held(from_step))
     smoothed = pl.pallas_call(
         functools.partial(edge_kernel, tiles),
         in_specs=[smem(), smem()] + [vmem()] * 5,

time: 38.4 us -> 37.5 us (0.977)
  waiting for transfers between devices: 2.63 us -> 1.56 us
    ppermute x1, waiting for transfers between devices: 1.95 us -> 0.01 us  [per_device(): from_step = lax.ppermute(step_edge, 'tiles', swaps(tiles, 1, False))]
    ppermute x1 -> x2, waiting for transfers between devices: 0.01 us -> 0.98 us  [the longest x1 0.98 us: per_device(): lax.ppermute(pair_edge, 'tiles', [p for p in pairs if p[0] % RING < RING...]
    ppermute x1 -> x2, starting transfers between devices: 1.91 us -> 2.59 us  [the longest x1 1.92 us: per_device(): lax.ppermute(pair_edge, 'tiles', [p for p in pairs if p[0] % RING < RING...]
    ppermute x1, starting transfers between devices: 15.5 us -> 14.8 us  [per_device(): from_step = lax.ppermute(step_edge, 'tiles', swaps(tiles, 1, False))]
  transfers between devices with their start and end apart: 4 -> 5, of which waited for: 2 -> 2; matrix products, arithmetic and copies ran while one was open for 0% -> 0% of each run, Pallas kernels for 7% -> 7%
where the time goes in v1:
time: 37.5 us; the launch traced here: 37.2 us
  starting transfers between devices  24.8 us (66%)
  Pallas kernels  10.2 us (27%)
  waiting for transfers between devices  1.56 us (4%)
  between operations  0.72 us (2%)
    ppermute x1, starting transfers between devices, per_device(): from_step = lax.ppermute(step_edge, 'tiles', swaps(tiles, 1, False))  14.8 us
    pallas_call x1, Pallas kernels, per_device(): pl.pallas_call(radiate_kernel, in_specs=[smem(), smem(), smem(), vmem(),...  5.48 us
    ppermute x1, starting transfers between devices, per_device(): far = lax.ppermute(to_far, 'band', swaps(bands, 1, True))  4 us
    ppermute x1, starting transfers between devices, per_device(): near = lax.ppermute(to_near, 'band', swaps(bands, 0, True))  3.4 us
    pallas_call x1, Pallas kernels, per_device(): pl.pallas_call(functools.partial(main_kernel, tiles), in_specs=[smem()] +...  2.46 us
    ppermute x1, starting transfers between devices, per_device(): lax.ppermute(pair_edge, 'tiles', [p for p in pairs if p[0] % RING < RING...  1.92 us
    pallas_call x1, Pallas kernels, per_device(): pl.pallas_call(functools.partial(edge_kernel, tiles), in_specs=[smem(), s...  1.72 us
    ppermute x1, waiting for transfers between devices, per_device(): lax.ppermute(pair_edge, 'tiles', [p for p in pairs if p[0] % RING < RING...  0.98 us
  transfers between devices with their start and end apart: 5, of which 2 were waited for; matrix products, arithmetic and copies ran while one was open for 0% of the time, Pallas kernels for 7%

profile of v1, /device:TPU:48, one launch (start us, length us, event | category | flops | bytes accessed | tf_op | source)
XLA Modules:
  0.0 37.2 jit_solution(2451125164183197027)
XLA Ops:
  0.6 5.5 %radiate.1 = (f32[90,16,128]{2,1,0:T(8,128)}, f32[90,16,128]{2,1,0:T(8,128)S(1)}, bf16[90,4,128]{2,1,0:T(4,128)(2,1)S(1)}, bf16[90,4,128]{2,1,0:T(4,128)(2,1)S(1)}) custom-call(s32[1]{0:T(128)} %bitcast.here_ref, f32[4]{0:T(128)} %weight_ref.1, s32[16]{0:T(128)} %bitcast.10, bf16[16,90,4,128]{3,2,1,0:T(4,128)(2,1)} %depth_ref.1, ...), custom_call_target="tpu_custom_call" | custom-call | tf_op jit(solution)/shard_map/radiate/pallas_call | solution.py:364
  6.1 14.8 %collective-permute-start.2 = (bf16[90,4,128]{2,1,0:T(4,128)(2,1)S(1)}, bf16[90,4,128]{2,1,0:T(4,128)(2,1)S(1)}, u32[]{:S(2)}, u32[]{:S(2)}) collective-permute-start(bf16[90,4,128]{2,1,0:T(4,128)(2,1)S(1)} %get-tuple-element.12), channel_id=1, source_target_pairs={{4,8},{8,4},{12,16},{16,12},{20,24},{24,20},{28,32},{32,28},{36,40... | collective-permute-start | bytes 276488 | tf_op jit(solution)/shard_map/ppermute | solution.py:378
  20.9 0.7 %collective-permute-start.1 = (bf16[90,4,128]{2,1,0:T(4,128)(2,1)S(1)}, bf16[90,4,128]{2,1,0:T(4,128)(2,1)S(1)}, u32[]{:S(2)}, u32[]{:S(2)}) collective-permute-start(bf16[90,4,128]{2,1,0:T(4,128)(2,1)S(1)} %get-tuple-element.11), channel_id=1, source_target_pairs={{48,52},{52,48},{56,60},{60,56},{64,68},{68,64},{72,76},{76,72},{8... | collective-permute-start | bytes 276488 | tf_op jit(solution)/shard_map/ppermute | solution.py:381
  21.6 1.9 %collective-permute-start = (bf16[90,4,128]{2,1,0:T(4,128)(2,1)S(1)}, bf16[90,4,128]{2,1,0:T(4,128)(2,1)S(1)}, u32[]{:S(2)}, u32[]{:S(2)}) collective-permute-start(bf16[90,4,128]{2,1,0:T(4,128)(2,1)S(1)} %get-tuple-element.11), channel_id=1, source_target_pairs={{0,4},{4,0},{8,12},{12,8},{16,20},{20,16},{24,28},{28,24},{32,36},... | collective-permute-start | bytes 276488 | tf_op jit(solution)/shard_map/ppermute | solution.py:380
  23.5 0.3 pack_own.1.own_ref
  23.8 0.0 collective-permute-done.2.step_ref
  23.8 0.0 collective-permute-done.1.late_ref
  23.8 1.0 %collective-permute-done.pair_ref = bf16[90,4,128]{2,1,0:T(4,128)(2,1)S(1)} collective-permute-done((bf16[90,4,128]{2,1,0:T(4,128)(2,1)S(1)}, bf16[90,4,128]{2,1,0:T(4,128)(2,1)S(1)}, u32[]{:S(2)}, u32[]{:S(2)}) %collective-permute-start) | collective-permute-done | bytes 92192 | tf_op jit(solution)/shard_map/ppermute | solution.py:380
  24.8 0.2 pack_outer.1
  25.0 3.4 %collective-permute-start.3 = (bf16[6,24,128]{2,1,0:T(8,128)(2,1)S(1)}, bf16[6,24,128]{2,1,0:T(8,128)(2,1)S(1)}, u32[]{:S(2)}, u32[]{:S(2)}) collective-permute-start(bf16[6,24,128]{2,1,0:T(8,128)(2,1)S(1)} %get-tuple-element.14), channel_id=1, source_target_pairs={{0,1},{1,0},{2,3},{3,2},{4,5},{5,4},{6,7},{7,6},{8,9},{9,8},{10,11... | collective-permute-start | bytes 110600 | tf_op jit(solution)/shard_map/ppermute | solution.py:397
  28.4 4.0 %collective-permute-start.4 = (bf16[6,24,128]{2,1,0:T(8,128)(2,1)S(1)}, bf16[6,24,128]{2,1,0:T(8,128)(2,1)S(1)}, u32[]{:S(2)}, u32[]{:S(2)}) collective-permute-start(bf16[6,24,128]{2,1,0:T(8,128)(2,1)S(1)} %get-tuple-element.15), channel_id=1, source_target_pairs={{1,2},{2,1},{3,0},{0,3},{5,6},{6,5},{7,4},{4,7},{9,10},{10,9},{11,... | collective-permute-start | bytes 110600 | tf_op jit(solution)/shard_map/ppermute | solution.py:398
  32.5 2.5 %inner.1.main_ref = f32[90,16,128]{2,1,0:T(8,128)S(1)} custom-call(s32[1]{0:T(128)} %bitcast.here_ref, f32[90,16,128]{2,1,0:T(8,128)S(1)} %get-tuple-element.10.field_ref, bf16[90,4,128]{2,1,0:T(4,128)(2,1)S(1)} %collective-permute-done.pair_ref, bf16[90,4,128]{2,1,0:T(4,128)(2,1)S(1)} %collective-permute-done.1.late_ref, ...), custom_call_target="tpu_custom_call" | custom-call | tf_op jit(solution)/shard_map/inner/pallas_call | solution.py:399
  34.9 0.0 collective-permute-done.3.near_ref
  34.9 0.6 %collective-permute-done.4.far_ref = bf16[6,24,128]{2,1,0:T(8,128)(2,1)S(1)} collective-permute-done((bf16[6,24,128]{2,1,0:T(8,128)(2,1)S(1)}, bf16[6,24,128]{2,1,0:T(8,128)(2,1)S(1)}, u32[]{:S(2)}, u32[]{:S(2)}) %collective-permute-start.4) | collective-permute-done | bytes 36896 | tf_op jit(solution)/shard_map/ppermute | solution.py:398
  35.5 1.7 %edge.1 = f32[90,16,128]{2,1,0:T(8,128)} custom-call(s32[1]{0:T(128)} %bitcast.here_ref, s32[1]{0:T(128)} %bitcast.5.side_ref, f32[12,16,128]{2,1,0:T(8,128)S(1)} %pack_own.1.own_ref, f32[12,8,128]{2,1,0:T(8,128)S(1)} %get-tuple-element.13.outer_ref, bf16[6,24,128]{2,1,0:T(8,128)(2,1)S(1)} %collective-permute-done.3.near_ref, ...), custom_call_target="tpu_custom_call" | custom-call | tf_op jit(solution)/shard_map/edge/pallas_call | solution.py:406
Async XLA Ops:
  6.1 17.7 %collective-permute-start.2 = (bf16[90,4,128]{2,1,0:T(4,128)(2,1)S(1)}, bf16[90,4,128]{2,1,0:T(4,128)(2,1)S(1)}, u32[]{:S(2)}, u32[]{:S(2)}) collective-permute-start(bf16[90,4,128]{2,1,0:T(4,128)(2,1)S(1)} %get-tuple-element.12), channel_id=1, source_target_pairs={{4,8},{8,4},{12,16},{16,12},{20,24},{24,20},{28,32},{32,28},{36,40... | collective-permute-start | bytes 276488 | tf_op jit(solution)/shard_map/ppermute | solution.py:378
  20.9 2.9 %collective-permute-start.1 = (bf16[90,4,128]{2,1,0:T(4,128)(2,1)S(1)}, bf16[90,4,128]{2,1,0:T(4,128)(2,1)S(1)}, u32[]{:S(2)}, u32[]{:S(2)}) collective-permute-start(bf16[90,4,128]{2,1,0:T(4,128)(2,1)S(1)} %get-tuple-element.11), channel_id=1, source_target_pairs={{48,52},{52,48},{56,60},{60,56},{64,68},{68,64},{72,76},{76,72},{8... | collective-permute-start | bytes 276488 | tf_op jit(solution)/shard_map/ppermute | solution.py:381
  21.6 3.2 %collective-permute-start = (bf16[90,4,128]{2,1,0:T(4,128)(2,1)S(1)}, bf16[90,4,128]{2,1,0:T(4,128)(2,1)S(1)}, u32[]{:S(2)}, u32[]{:S(2)}) collective-permute-start(bf16[90,4,128]{2,1,0:T(4,128)(2,1)S(1)} %get-tuple-element.11), channel_id=1, source_target_pairs={{0,4},{4,0},{8,12},{12,8},{16,20},{20,16},{24,28},{28,24},{32,36},... | collective-permute-start | bytes 276488 | tf_op jit(solution)/shard_map/ppermute | solution.py:380
  25.0 9.9 %collective-permute-start.3 = (bf16[6,24,128]{2,1,0:T(8,128)(2,1)S(1)}, bf16[6,24,128]{2,1,0:T(8,128)(2,1)S(1)}, u32[]{:S(2)}, u32[]{:S(2)}) collective-permute-start(bf16[6,24,128]{2,1,0:T(8,128)(2,1)S(1)} %get-tuple-element.14), channel_id=1, source_target_pairs={{0,1},{1,0},{2,3},{3,2},{4,5},{5,4},{6,7},{7,6},{8,9},{9,8},{10,11... | collective-permute-start | bytes 110600 | tf_op jit(solution)/shard_map/ppermute | solution.py:397
  28.4 7.1 %collective-permute-start.4 = (bf16[6,24,128]{2,1,0:T(8,128)(2,1)S(1)}, bf16[6,24,128]{2,1,0:T(8,128)(2,1)S(1)}, u32[]{:S(2)}, u32[]{:S(2)}) collective-permute-start(bf16[6,24,128]{2,1,0:T(8,128)(2,1)S(1)} %get-tuple-element.15), channel_id=1, source_target_pairs={{1,2},{2,1},{3,0},{0,3},{5,6},{6,5},{7,4},{4,7},{9,10},{10,9},{11,... | collective-permute-start | bytes 110600 | tf_op jit(solution)/shard_map/ppermute | solution.py:398
